TPU v7x, 256 devices: a whole 4x4x8 slice. The times are simulated.
256 devices in a mesh: dp: 16 (over y, x), vocab: 16 (over z, core).
Axes of the slice: x: 4, y: 4, z: 8, core: 2. Of those that a mesh axis runs over, the one named last changes fastest.
Arguments:
- hidden: bfloat16 [256, 128, 4096], P('vocab', None, 'dp'), may hold values from -6 to 6
- weights: bfloat16 [65536, 4096], P('vocab', 'dp'), may hold values from -0.09375 to 0.09375
- bias: float32 [65536], P('vocab'), may hold values from -4 to 4
- first_moment: bfloat16 [65536, 4096], P('vocab', 'dp'), may hold values from -6 to 6
- second_moment: bfloat16 [65536, 4096], P('vocab', 'dp'), may hold values from 0.049804688 to 2
- rep_cot: bfloat16 [256, 16, 512], P(None, 'vocab'), may hold values from -768 to 768
- active_blocks: int32 [256, 16, 4], P(None, 'vocab'), may hold values from 0 to 31, as said below
- block_counts: int32 [256, 16], replicated, may hold values from 0 to 4, as said below
- passage_len: int32 [256], replicated, may hold values from 16 to 128, as said below
Outputs:
- reps: float32 [16, 16, 4, 512], P('dp', 'vocab')
- grad_hidden: bfloat16 [256, 128, 4096], P('vocab', None, 'dp')
- new_first: bfloat16 [65536, 4096], P('vocab', 'dp')
- new_second: bfloat16 [65536, 4096], P('vocab', 'dp')
Inputs may be any that keep to these rules, and one draw needn't show every extreme that they name: `block_counts`: within each batch of 16 passages, every owner has between max(1, 2) and 4 live passages, and in every batch some owner has exactly 4; some passage at each owner of each batch has count 4. `active_blocks`: the 4 block numbers of one passage at one owner are distinct. `passage_len`: every batch has a passage of length 128.
All inputs are finite; a program needn't handle non-finite values.
Results may differ from a plain program's by a relative error of at most 0.012.
Values may be sent and summed in bfloat16 or wider, within the bound.
No kernel may reach another device: no remote copies, remote signals or barrier semaphores. Data moves between devices by JAX's collectives and lax.ppermute only.
A program may use at most 128 MiB of HBM per device.

v0:
```python
import jax
import jax.numpy as jnp
from jax import lax
from jax.sharding import PartitionSpec as P

BLOCK = 128
OWN_BLOCKS = 32
SLOT_BLOCKS = 4
OWN_SLOTS = 4
beta_one = 0.9
beta_two = 0.999


def slot_tables(block_counts, batches, owners, per_batch, slot_total):
    live_mask = (block_counts > 0).astype(jnp.int32).reshape(batches, per_batch, owners)
    slot_rank = jnp.cumsum(live_mask, axis=1, dtype=jnp.int32) - live_mask
    slot_place = jnp.arange(slot_total, dtype=jnp.int32)
    chosen = (live_mask[:, :, :, None] == 1) & (
        slot_rank[:, :, :, None] == slot_place[None, None, None, :]
    )
    return jnp.transpose(chosen, (0, 2, 3, 1)).astype(jnp.int32)


def slot_info(onehot, ids_col, counts_col, lengths, plen_size, block_size):
    slot_ids = jnp.sum(onehot[:, :, :, None] * ids_col[:, None, :, :], axis=2)
    slot_count = jnp.sum(onehot * counts_col[:, None, :], axis=2)
    slot_len = jnp.sum(onehot * lengths[:, None, :], axis=2)
    filled = jnp.sum(onehot, axis=2)
    divisor = jnp.where(filled > 0, slot_len, 1).astype(jnp.float32)
    token_ok = jnp.arange(plen_size, dtype=jnp.int32)[None, None, :] < slot_len[:, :, None]
    col_block = jnp.arange(slot_ids.shape[2] * block_size, dtype=jnp.int32) // block_size
    col_ok = col_block[None, None, :] < slot_count[:, :, None]
    return (slot_ids, divisor, token_ok, col_ok)


def activate(logits, bias_cols, cot, token_ok, col_ok, divisor):
    shifted = logits + bias_cols[:, :, None, :]
    softened = jax.nn.softplus(shifted)
    kept_mask = (token_ok[:, :, :, None] & col_ok[:, :, None, :]).astype(jnp.float32)
    pool_weight = kept_mask / divisor[:, :, None, None]
    pooled = jnp.sum(jnp.log1p(softened) * pool_weight, axis=2)
    slope = (cot[:, :, None, :] * pool_weight * jax.nn.sigmoid(shifted) / (1.0 + softened)).astype(
        jnp.bfloat16
    )
    return (pooled, slope)


def shards(
    hidden,
    weights,
    bias,
    first_moment,
    second_moment,
    rep_cot,
    active_blocks,
    block_counts,
    passage_len,
):
    owners = lax.axis_size("vocab")
    feature_parts = lax.axis_size("dp")
    per_batch, plen_size, dslice = hidden.shape
    col_width = SLOT_BLOCKS * BLOCK
    my_batch = lax.axis_index("vocab")
    chosen = slot_tables(block_counts, owners, owners, per_batch, OWN_SLOTS)
    my_slots = lax.dynamic_index_in_dim(chosen, my_batch, 0, keepdims=False)
    pick_rows = my_slots.reshape(owners * OWN_SLOTS, per_batch).astype(jnp.bfloat16)
    outgoing = jnp.dot(
        pick_rows, hidden.reshape(per_batch, plen_size * dslice), preferred_element_type=jnp.float32
    )
    outgoing = outgoing.astype(jnp.bfloat16).reshape(owners, OWN_SLOTS, plen_size, dslice)
    arrived = lax.all_to_all(outgoing, "vocab", split_axis=0, concat_axis=0, tiled=True)
    onehot = lax.dynamic_index_in_dim(chosen, my_batch, 1, keepdims=False)
    ids_col = active_blocks.reshape(owners, per_batch, SLOT_BLOCKS)
    counts_col = lax.dynamic_index_in_dim(block_counts, my_batch, 1, keepdims=False).reshape(
        owners, per_batch
    )
    lengths = passage_len.reshape(owners, per_batch)
    slot_ids, divisor, token_ok, col_ok = slot_info(
        onehot, ids_col, counts_col, lengths, plen_size, BLOCK
    )
    cot_col = rep_cot.reshape(owners, per_batch, col_width).astype(jnp.float32)
    slot_cot = jnp.einsum("jsp,jpc->jsc", onehot.astype(jnp.float32), cot_col)
    w_blocks = weights.reshape(OWN_BLOCKS, BLOCK, dslice)
    bias_blocks = bias.reshape(OWN_BLOCKS, BLOCK)
    bias_cols = bias_blocks[slot_ids].reshape(owners, OWN_SLOTS, col_width)

    def partial_for(inputs_here):
        slot_rows, block_ids = inputs_here
        w_sel = w_blocks[block_ids].reshape(OWN_SLOTS, col_width, dslice)
        return jnp.einsum(
            "std,scd->stc", slot_rows, w_sel, preferred_element_type=jnp.float32
        ).astype(jnp.bfloat16)

    partial_value = lax.map(partial_for, (arrived, slot_ids))
    my_share = owners // feature_parts
    my_start = lax.axis_index("dp") * my_share
    logits_mine = lax.psum_scatter(partial_value, "dp", scatter_dimension=0, tiled=True).astype(
        jnp.float32
    )
    pooled_mine, slope_mine = activate(
        logits_mine,
        lax.dynamic_slice_in_dim(bias_cols, my_start, my_share, 0),
        lax.dynamic_slice_in_dim(slot_cot, my_start, my_share, 0),
        lax.dynamic_slice_in_dim(token_ok, my_start, my_share, 0),
        lax.dynamic_slice_in_dim(col_ok, my_start, my_share, 0),
        lax.dynamic_slice_in_dim(divisor, my_start, my_share, 0),
    )
    slope_all = lax.all_gather(slope_mine, "dp", axis=0, tiled=True)

    def backward_step(grad_sum, inputs_here):
        slot_rows, block_ids, slope = inputs_here
        w_sel = w_blocks[block_ids].reshape(OWN_SLOTS, col_width, dslice)
        back_part = jnp.einsum(
            "stc,scd->std", slope, w_sel, preferred_element_type=jnp.float32
        ).astype(jnp.bfloat16)
        outer_sum = jnp.einsum("std,stc->scd", slot_rows, slope, preferred_element_type=jnp.float32)
        grad_sum = grad_sum.at[block_ids.reshape(-1)].add(
            outer_sum.reshape(OWN_SLOTS * SLOT_BLOCKS, BLOCK, dslice)
        )
        return (grad_sum, back_part)

    start_grad = jnp.zeros((OWN_BLOCKS, BLOCK, dslice), jnp.float32)
    grad_blocks, returned = lax.scan(backward_step, start_grad, (arrived, slot_ids, slope_all))
    back_home = lax.all_to_all(returned, "vocab", split_axis=0, concat_axis=0, tiled=True)
    gathered = jnp.dot(
        pick_rows.T,
        back_home.reshape(owners * OWN_SLOTS, plen_size * dslice),
        preferred_element_type=jnp.float32,
    )
    grad_hidden = gathered.reshape(per_batch, plen_size, dslice).astype(jnp.bfloat16)
    grad_w = grad_blocks.reshape(OWN_BLOCKS * BLOCK, dslice)
    new_first = (beta_one * first_moment.astype(jnp.float32) + (1.0 - beta_one) * grad_w).astype(
        jnp.bfloat16
    )
    new_second = (
        beta_two * second_moment.astype(jnp.float32) + (1.0 - beta_two) * grad_w * grad_w
    ).astype(jnp.bfloat16)
    reps = pooled_mine[:, None, :, :]
    return (reps, grad_hidden, new_first, new_second)


def solution(mesh):
    return jax.shard_map(
        shards,
        mesh=mesh,
        in_specs=(
            P("vocab", None, "dp"),
            P("vocab", "dp"),
            P("vocab"),
            P("vocab", "dp"),
            P("vocab", "dp"),
            P(None, "vocab", None),
            P(None, "vocab", None),
            P(),
            P(),
        ),
        out_specs=(
            P("dp", "vocab", None, None),
            P("vocab", None, "dp"),
            P("vocab", "dp"),
            P("vocab", "dp"),
        ),
        check_vma=False,
    )
```

profile of v0, /device:TPU:1, one launch (start us, length us, event | category | flops | bytes accessed | tf_op | source)
XLA Modules:
  0.0 653.8 jit_solution(12631458405986258486)
XLA Ops:
  12.3 3.0 copy.65
  15.3 10.1 %all-to-all-start = ((bf16[16,4,128,256]{3,2,1,0:T(8,128)(2,1)}), bf16[16,4,128,256]{3,2,1,0:T(8,128)(2,1)}, u32[]{:S(2)}, u32[]{:S(2)}) async-start(bf16[16,4,128,256]{3,2,1,0:T(8,128)(2,1)} %bitcast.132), calls=%async_computation | async-start | bytes 8388608 | tf_op jit(solution)/shard_map/all_to_all | solution.py:71
  27.6 91.4 %all-to-all-done = bf16[16,4,128,256]{3,2,1,0:T(8,128)(2,1)} async-done(((bf16[16,4,128,256]{3,2,1,0:T(8,128)(2,1)}), bf16[16,4,128,256]{3,2,1,0:T(8,128)(2,1)}, u32[]{:S(2)}, u32[]{:S(2)}) %all-to-all-start) | async-done | bytes 4194336 | tf_op jit(solution)/shard_map/all_to_all | solution.py:71
  119.0 78.0 %while.22 = (s32[]{:T(128)}, bf16[16,4,128,512]{2,3,1,0:T(8,128)(2,1)}, bf16[16,4,128,256]{3,2,1,0:T(8,128)(2,1)}, s32[16,4,4]{2,1,0:T(4,128)S(1)}, bf16[32,128,256]{2,1,0:T(8,128)(2,1)}, /*index=5*/s32[]{:T(128)}) while((s32[]{:T(128)}, bf16[16,4,128,512]{2,3,1,0:T(8,128)(2,1)}, bf16[16,4,128,256]{3,2,1,0:T(8,128)(2,1)}, ...), condition=%wide.region_3.4_spmd, body=%wide.region_2.3_spmd.sunk | while | flops 134480944 | bytes 6033881 | solution.py:94
  119.1 2.2 gather_fusion
  123.9 2.2 gather_fusion
  128.8 2.2 gather_fusion
  143.4 2.2 gather_fusion
  148.3 2.2 gather_fusion
  158.0 2.2 gather_fusion
  162.9 2.2 gather_fusion
  192.2 2.2 gather_fusion
  199.2 86.7 %reduce-scatter.4.cloned.1.call-done = bf16[1,4,128,512]{2,3,1,0:T(8,128)(2,1)} async-done(((bf16[16,4,128,512]{2,3,1,0:T(8,128)(2,1)}), bf16[1,4,128,512]{2,3,1,0:T(8,128)(2,1)}) %reduce-scatter.4.cloned.1.call-update) | async-done | bytes 524304
  285.9 4.0 divide_convert_fusion
  291.0 76.7 %all-gather.2.cloned.1.call-done = bf16[16,4,128,512]{3,2,1,0:T(8,128)(2,1)} async-done(((bf16[1,4,128,512]{3,2,1,0:T(8,128)(2,1)}), bf16[16,4,128,512]{3,2,1,0:T(8,128)(2,1)}) %all-gather.2.cloned.1.call-update) | async-done | bytes 8388624 | tf_op jit(solution)/shard_map/all_gather | solution.py:108
  367.6 2.4 broadcast_in_dim.23
  370.1 168.9 %while.23 = (s32[]{:T(128)}, f32[32,128,256]{2,1,0:T(8,128)}, bf16[16,4,128,256]{3,2,1,0:T(8,128)(2,1)}, s32[16,4,4]{2,1,0:T(4,128)S(1)}, bf16[16,4,128,512]{3,2...) while((s32[]{:T(128)}, f32[32,128,256]{2,1,0:T(8,128)}, ...), condition=%wide.region_11.12_spmd, body=%wide.region_9.11_spmd.sunk | while | flops 269091936 | bytes 13114209 | solution.py:123
  371.8 4.5 scatter_fusion
  376.4 2.2 gather_fusion.1
  382.3 4.4 scatter_fusion
  386.9 2.2 gather_fusion.1
  392.8 4.6 scatter_fusion
  397.5 2.2 gather_fusion.1
  403.5 4.6 scatter_fusion
  408.2 2.2 gather_fusion.1
  414.2 4.4 scatter_fusion
  418.6 2.2 gather_fusion.1
  424.6 4.5 scatter_fusion
  429.2 2.2 gather_fusion.1
  435.2 4.5 scatter_fusion
  445.7 4.6 scatter_fusion
  456.4 4.5 scatter_fusion
  460.9 2.2 gather_fusion.1
  466.9 4.5 scatter_fusion
  471.5 2.2 gather_fusion.1
  477.5 4.5 scatter_fusion
  482.1 2.2 gather_fusion.1
  488.1 4.6 scatter_fusion
  492.7 2.2 gather_fusion.1
  498.7 4.5 scatter_fusion
  509.2 4.5 scatter_fusion
  519.8 4.4 scatter_fusion
  524.2 2.2 gather_fusion.1
  530.2 4.4 scatter_fusion
  539.0 8.6 %all-to-all-start.1 = ((bf16[16,4,128,256]{3,2,1,0:T(8,128)(2,1)}), bf16[16,4,128,256]{3,2,1,0:T(8,128)(2,1)}, u32[]{:S(2)}, u32[]{:S(2)}) async-start(bf16[16,4,128,256]{3,2,1,0:T(8,128)(2,1)} %get-tuple-element.70), calls=%async_computation.1 | async-start | bytes 8388608 | tf_op jit(solution)/shard_map/all_to_all | solution.py:124
  547.6 6.3 fusion.17
  553.9 87.2 %all-to-all-done.1 = bf16[16,4,128,256]{3,2,1,0:T(8,128)(2,1)} async-done(((bf16[16,4,128,256]{3,2,1,0:T(8,128)(2,1)}), bf16[16,4,128,256]{3,2,1,0:T(8,128)(2,1)}, u32[]{:S(2)}, u32[]{:S(2)}) %all-to-all-start.1) | async-done | bytes 4194336 | tf_op jit(solution)/shard_map/all_to_all | solution.py:124
  641.1 4.5 fusion.23
  (271 shorter events, 144.1 us)
Async XLA Ops:
  7.2 191.7 %copy-start = (bf16[256,1,512]{2,0,1:T(8,128)(2,1)S(1)}, bf16[256,1,512]{2,0,1:T(8,128)(2,1)}, u32[]{:S(2)}) copy-start(bf16[256,1,512]{2,0,1:T(8,128)(2,1)} %param.18) | copy-start | bytes 786436
  15.3 10.2 %copy-start.3 = (s32[256,1,4]{0,2,1:T(4,128)S(1)}, s32[256,1,4]{0,2,1:T(4,128)}, u32[]{:S(2)}) copy-start(s32[256,1,4]{0,2,1:T(4,128)} %param.19) | copy-start | bytes 12292
  15.3 11.0 %copy-start.4 = (s32[256]{0:T(256)S(1)}, s32[256]{0:T(256)}, u32[]{:S(2)}) copy-start(s32[256]{0:T(256)} %param.21) | copy-start | bytes 3076
  15.3 103.6 %all-to-all-start = ((bf16[16,4,128,256]{3,2,1,0:T(8,128)(2,1)}), bf16[16,4,128,256]{3,2,1,0:T(8,128)(2,1)}, u32[]{:S(2)}, u32[]{:S(2)}) async-start(bf16[16,4,128,256]{3,2,1,0:T(8,128)(2,1)} %bitcast.132), calls=%async_computation | async-start | bytes 8388608 | tf_op jit(solution)/shard_map/all_to_all | solution.py:71
  25.4 260.5 %reduce-scatter.4.cloned.1.call-start = ((), (), s32[]{:S(2)}) async-start(), calls=%async_computation.4 | async-start | bytes 8912896
  196.9 0.7 copy-start.1
  197.0 170.7 %all-gather.2.cloned.1.call-start = ((), (), s32[]{:S(2)}) async-start(), calls=%async_computation.3 | async-start | bytes 8912896 | tf_op jit(solution)/shard_map/all_gather | solution.py:108
  539.0 8.6 %copy-start.2 = (bf16[4096,256]{1,0:T(8,128)(2,1)S(1)}, bf16[4096,256]{1,0:T(8,128)(2,1)}, u32[]{:S(2)}) copy-start(bf16[4096,256]{1,0:T(8,128)(2,1)} %param.17) | copy-start | bytes 6291460
  539.0 102.1 %all-to-all-start.1 = ((bf16[16,4,128,256]{3,2,1,0:T(8,128)(2,1)}), bf16[16,4,128,256]{3,2,1,0:T(8,128)(2,1)}, u32[]{:S(2)}, u32[]{:S(2)}) async-start(bf16[16,4,128,256]{3,2,1,0:T(8,128)(2,1)} %get-tuple-element.70), calls=%async_computation.1 | async-start | bytes 8388608 | tf_op jit(solution)/shard_map/all_to_all | solution.py:124
Sparse Core Ops, SparseCore 0:
  197.1 88.7 reduce-scatter.3
  291.1 76.5 all-gather.1
where the time goes:
time: 657 us; the launch traced here: 654 us
  waiting for transfers between devices  342 us (52%)
  local copies, waits for them, and re-layouts  105 us (16%)
  matrix products  87.3 us (13%)
  other arithmetic  85.8 us (13%)
  starting transfers between devices  18.8 us (3%)
  between operations  14.2 us (2%)
    all_to_all x1, waiting for transfers between devices, shards(): lax.all_to_all(outgoing, 'vocab', split_axis=0, concat_axis=0, tiled=True)  91.4 us
    all_to_all x1, waiting for transfers between devices, shards(): lax.all_to_all(returned, 'vocab', split_axis=0, concat_axis=0, tiled=True)  87.2 us
    unnamed x3, waiting for transfers between devices  86.8 us
    all_gather x1, waiting for transfers between devices, shards(): slope_all = lax.all_gather(slope_mine, 'dp', axis=0, tiled=True)  76.7 us
    scatter-add x16, other arithmetic, backward_step(): grad_sum.at[block_ids.reshape(-1)]  71.8 us
    gather x16, local copies, waits for them, and re-layouts, partial_for(): w_sel = w_blocks[block_ids].reshape(OWN_SLOTS, col_width, dslice)  35.3 us
    gather x16, local copies, waits for them, and re-layouts, backward_step(): w_sel = w_blocks[block_ids].reshape(OWN_SLOTS, col_width, dslice)  35.3 us
    dot_general x16, matrix products, backward_step(): jnp.einsum('stc,scd->std', slope, w_sel, preferred_element_type=jnp.float32)  33.1 us
  transfers between devices with their start and end apart: 4, of which 4 were waited for; matrix products, arithmetic and copies ran while one was open for 2% of the time, Pallas kernels for 0%

commit v1 on v0

--- a/solution.py
+++ b/solution.py
@@ -105,7 +105,8 @@
         lax.dynamic_slice_in_dim(col_ok, my_start, my_share, 0),
         lax.dynamic_slice_in_dim(divisor, my_start, my_share, 0),
     )
-    slope_all = lax.all_gather(slope_mine, "dp", axis=0, tiled=True)
+    outgoing_2 = jnp.stack([slope_mine] * lax.axis_size("dp"))
+    slope_all = jnp.concatenate(lax.all_to_all(outgoing_2, "dp", 0, 0), axis=0)
 
     def backward_step(grad_sum, inputs_here):
         slot_rows, block_ids, slope = inputs_here

time: 657 us -> 707 us (1.076)
  waiting for transfers between devices: 342 us -> 386 us
  local copies, waits for them, and re-layouts: 105 us -> 91.6 us
  matrix products: 87.3 us -> 99.7 us
  starting transfers between devices: 18.8 us -> 26.4 us
    all_to_all x0 -> x1, waiting for transfers between devices: none -> 121 us  [shards(): slope_all = jnp.concatenate(lax.all_to_all(outgoing_2, 'dp', 0, 0), axis=0)]
    all_gather x1 -> x0, waiting for transfers between devices: 76.7 us -> none  [shards(): slope_all = lax.all_gather(slope_mine, 'dp', axis=0, tiled=True)]
    dynamic_update_slice x32 -> x0, local copies, waits for them, and re-layouts: 17.9 us -> none  [shards(): partial_value = lax.map(partial_for, (arrived, slot_ids))]
    dot_general x16, matrix products: 22.9 us -> 35.8 us  [partial_for(): jnp.einsum('std,scd->stc', slot_rows, w_sel, preferred_element_type=jnp.f...]
    unnamed x3 -> x2, waiting for transfers between devices: 86.8 us -> 86.6 us
  transfers between devices with their start and end apart: 4 -> 4, of which waited for: 4 -> 4; matrix products, arithmetic and copies ran while one was open for 2% -> 1% of each run, Pallas kernels for 0% -> 0%
where the time goes in v1:
time: 707 us; the launch traced here: 704 us
  waiting for transfers between devices  386 us (55%)
  matrix products  99.7 us (14%)
  local copies, waits for them, and re-layouts  91.6 us (13%)
  other arithmetic  85.5 us (12%)
  starting transfers between devices  26.4 us (4%)
  between operations  14.3 us (2%)
    all_to_all x1, waiting for transfers between devices, shards(): slope_all = jnp.concatenate(lax.all_to_all(outgoing_2, 'dp', 0, 0), axis=0)  121 us
    all_to_all x1, waiting for transfers between devices, shards(): lax.all_to_all(outgoing, 'vocab', split_axis=0, concat_axis=0, tiled=True)  91.4 us
    all_to_all x1, waiting for transfers between devices, shards(): lax.all_to_all(returned, 'vocab', split_axis=0, concat_axis=0, tiled=True)  87.2 us
    unnamed x2, waiting for transfers between devices  86.6 us
    scatter-add x16, other arithmetic, backward_step(): grad_sum.at[block_ids.reshape(-1)]  72.3 us
    dot_general x16, matrix products, partial_for(): jnp.einsum('std,scd->stc', slot_rows, w_sel, preferred_element_type=jnp.f...  35.8 us
    gather x16, local copies, waits for them, and re-layouts, partial_for(): w_sel = w_blocks[block_ids].reshape(OWN_SLOTS, col_width, dslice)  35.3 us
    gather x16, local copies, waits for them, and re-layouts, backward_step(): w_sel = w_blocks[block_ids].reshape(OWN_SLOTS, col_width, dslice)  35.3 us
  transfers between devices with their start and end apart: 4, of which 4 were waited for; matrix products, arithmetic and copies ran while one was open for 1% of the time, Pallas kernels for 0%

profile of v1, /device:TPU:1, one launch (start us, length us, event | category | flops | bytes accessed | tf_op | source)
XLA Modules:
  0.0 703.7 jit_solution(12581342079753632725)
XLA Ops:
  12.3 3.1 copy.58
  15.4 10.1 %all-to-all-start = ((bf16[16,4,128,256]{3,2,1,0:T(8,128)(2,1)}), bf16[16,4,128,256]{3,2,1,0:T(8,128)(2,1)}, u32[]{:S(2)}, u32[]{:S(2)}) async-start(bf16[16,4,128,256]{3,2,1,0:T(8,128)(2,1)} %bitcast.135), calls=%async_computation | async-start | bytes 8388608 | tf_op jit(solution)/shard_map/all_to_all | solution.py:71
  27.6 91.4 %all-to-all-done = bf16[16,4,128,256]{3,2,1,0:T(8,128)(2,1)} async-done(((bf16[16,4,128,256]{3,2,1,0:T(8,128)(2,1)}), bf16[16,4,128,256]{3,2,1,0:T(8,128)(2,1)}, u32[]{:S(2)}, u32[]{:S(2)}) %all-to-all-start) | async-done | bytes 4194336 | tf_op jit(solution)/shard_map/all_to_all | solution.py:71
  119.0 72.8 %while.22 = (s32[]{:T(128)}, bf16[16,4,128,512]{3,2,1,0:T(8,128)(2,1)}, bf16[16,4,128,256]{3,2,1,0:T(8,128)(2,1)}, s32[16,4,4]{2,1,0:T(4,128)S(1)}, bf16[32,128,256]{2,1,0:T(8,128)(2,1)}, /*index=5*/s32[]{:T(128)}) while((s32[]{:T(128)}, bf16[16,4,128,512]{3,2,1,0:T(8,128)(2,1)}, bf16[16,4,128,256]{3,2,1,0:T(8,128)(2,1)}, ...), condition=%wide.region_3.4_spmd, body=%wide.region_2.3_spmd.sunk | while | flops 134480944 | bytes 3937737 | solution.py:94
  119.1 2.2 gather_fusion
  121.3 2.2 fusion.59
  125.8 2.2 fusion.59
  130.4 2.3 fusion.59
  134.9 2.2 fusion.59
  139.5 2.2 fusion.59
  144.0 2.2 fusion.59
  148.6 2.2 fusion.59
  153.1 2.2 fusion.59
  157.7 2.2 fusion.59
  162.2 2.3 fusion.59
  166.8 2.2 fusion.59
  171.3 2.2 fusion.59
  175.9 2.2 fusion.59
  180.4 2.3 fusion.59
  185.0 2.2 fusion.59
  189.5 2.2 fusion.59
  194.0 86.6 %reduce-scatter.4.cloned.1.call-done = bf16[1,4,128,512]{3,2,1,0:T(8,128)(2,1)} async-done(((bf16[16,4,128,512]{3,2,1,0:T(8,128)(2,1)}), bf16[1,4,128,512]{3,2,1,0:T(8,128)(2,1)}) %reduce-scatter.4.cloned.1.call-update) | async-done | bytes 524304
  280.5 3.1 fusion.28
  283.9 5.2 stack.2
  289.1 4.7 all-to-all-start.1
  293.9 120.7 %all-to-all-done.1 = bf16[16,1,4,128,512]{3,4,2,1,0:T(8,128)(2,1)} async-done(((bf16[16,1,4,128,512]{3,4,2,1,0:T(8,128)(2,1)}), bf16[16,1,4,128,512]{3,4,2,1,0:T(8,128)(2,1)}, u32[]{:S(2)}, u32[]{:S(2)}) %all-to-all-start.1) | async-done | bytes 8388640 | tf_op jit(solution)/shard_map/all_to_all | solution.py:109
  414.6 2.5 broadcast_in_dim.23
  417.0 169.0 %while.23 = (s32[]{:T(128)}, f32[32,128,256]{2,1,0:T(8,128)}, bf16[16,4,128,256]{3,2,1,0:T(8,128)(2,1)}, s32[16,4,4]{2,1,0:T(4,128)S(1)}, bf16[16,4,128,512]{2,3...) while((s32[]{:T(128)}, f32[32,128,256]{2,1,0:T(8,128)}, ...), condition=%wide.region_11.12_spmd, body=%wide.region_9.11_spmd.sunk | while | flops 269091936 | bytes 13114201 | solution.py:124
  418.7 4.5 scatter_fusion
  429.2 4.4 scatter_fusion
  439.7 4.7 scatter_fusion
  450.4 4.7 scatter_fusion
  461.2 4.4 scatter_fusion
  471.6 4.4 scatter_fusion
  482.1 4.5 scatter_fusion
  492.7 4.6 scatter_fusion
  503.3 4.5 scatter_fusion
  513.9 4.5 scatter_fusion
  524.4 4.6 scatter_fusion
  535.0 4.6 scatter_fusion
  545.6 4.6 scatter_fusion
  556.3 4.5 scatter_fusion
  566.8 4.4 scatter_fusion
  577.2 4.4 scatter_fusion
  586.0 11.5 %all-to-all-start.2 = ((bf16[16,4,128,256]{3,2,1,0:T(8,128)(2,1)}), bf16[16,4,128,256]{3,2,1,0:T(8,128)(2,1)}, u32[]{:S(2)}, u32[]{:S(2)}) async-start(bf16[16,4,128,256]{3,2,1,0:T(8,128)(2,1)} %get-tuple-element.70), calls=%async_computation.2 | async-start | bytes 8388608 | tf_op jit(solution)/shard_map/all_to_all | solution.py:125
  597.5 6.3 fusion.18
  603.8 87.2 %all-to-all-done.2 = bf16[16,4,128,256]{3,2,1,0:T(8,128)(2,1)} async-done(((bf16[16,4,128,256]{3,2,1,0:T(8,128)(2,1)}), bf16[16,4,128,256]{3,2,1,0:T(8,128)(2,1)}, u32[]{:S(2)}, u32[]{:S(2)}) %all-to-all-start.2) | async-done | bytes 4194336 | tf_op jit(solution)/shard_map/all_to_all | solution.py:125
  691.0 4.5 fusion.24
  (241 shorter events, 141.8 us)
Async XLA Ops:
  7.2 186.5 %copy-start = (bf16[256,1,512]{2,0,1:T(8,128)(2,1)S(1)}, bf16[256,1,512]{2,0,1:T(8,128)(2,1)}, u32[]{:S(2)}) copy-start(bf16[256,1,512]{2,0,1:T(8,128)(2,1)} %param.18) | copy-start | bytes 786436
  15.3 11.0 %copy-start.5 = (s32[256]{0:T(256)S(1)}, s32[256]{0:T(256)}, u32[]{:S(2)}) copy-start(s32[256]{0:T(256)} %param.21) | copy-start | bytes 3076
  15.4 11.7 %copy-start.4 = (s32[256,1,4]{0,2,1:T(4,128)S(1)}, s32[256,1,4]{0,2,1:T(4,128)}, u32[]{:S(2)}) copy-start(s32[256,1,4]{0,2,1:T(4,128)} %param.19) | copy-start | bytes 12292
  15.4 103.6 %all-to-all-start = ((bf16[16,4,128,256]{3,2,1,0:T(8,128)(2,1)}), bf16[16,4,128,256]{3,2,1,0:T(8,128)(2,1)}, u32[]{:S(2)}, u32[]{:S(2)}) async-start(bf16[16,4,128,256]{3,2,1,0:T(8,128)(2,1)} %bitcast.135), calls=%async_computation | async-start | bytes 8388608 | tf_op jit(solution)/shard_map/all_to_all | solution.py:71
  25.5 255.1 %reduce-scatter.4.cloned.1.call-start = ((), (), s32[]{:S(2)}) async-start(), calls=%async_computation.4 | async-start | bytes 8912896
  191.8 0.7 copy-start.2
  289.1 125.4 %all-to-all-start.1 = ((bf16[16,1,4,128,512]{3,4,2,1,0:T(8,128)(2,1)}), bf16[16,1,4,128,512]{3,4,2,1,0:T(8,128)(2,1)}, u32[]{:S(2)}, u32[]{:S(2)}) async-start(bf16[16,1,4,128,512]{3,4,2,1,0:T(8,128)(2,1)} %stack.2), calls=%async_computation.1 | async-start | bytes 16777216 | tf_op jit(solution)/shard_map/all_to_all | solution.py:109
  586.0 11.5 %copy-start.3 = (bf16[4096,256]{1,0:T(8,128)(2,1)S(1)}, bf16[4096,256]{1,0:T(8,128)(2,1)}, u32[]{:S(2)}) copy-start(bf16[4096,256]{1,0:T(8,128)(2,1)} %param.17) | copy-start | bytes 6291460
  586.0 105.0 %all-to-all-start.2 = ((bf16[16,4,128,256]{3,2,1,0:T(8,128)(2,1)}), bf16[16,4,128,256]{3,2,1,0:T(8,128)(2,1)}, u32[]{:S(2)}, u32[]{:S(2)}) async-start(bf16[16,4,128,256]{3,2,1,0:T(8,128)(2,1)} %get-tuple-element.70), calls=%async_computation.2 | async-start | bytes 8388608 | tf_op jit(solution)/shard_map/all_to_all | solution.py:125
  597.5 99.4 %copy-start.1 = (bf16[256,1,512]{2,0,1:T(8,128)(2,1)S(1)}, bf16[256,1,512]{2,0,1:T(8,128)(2,1)}, u32[]{:S(2)}) copy-start(bf16[256,1,512]{2,0,1:T(8,128)(2,1)} %param.18) | copy-start | bytes 786436
Sparse Core Ops, SparseCore 0:
  191.9 88.5 reduce-scatter.3
